TPU v7x, 256 devices: a whole 4x4x8 slice. The times are simulated.
256 devices in a mesh: slab: 64 (over y, z, x_lo), ffn: 4 (over x_hi, core).
Axes of the slice: x: 4 (x_hi: 2, x_lo: 2; x = x_hi * 2 + x_lo), y: 4, z: 8, core: 2. Of those that a mesh axis runs over, the one named last changes fastest.
Arguments:
- tokens: bfloat16 [32768, 512], P('slab'), may hold values from -6 to 6
- gain_attn: float32 [512], replicated, may hold values from 0.1 to 1.9
- w_reduce: bfloat16 [4096, 512], replicated, may hold values from -0.09375 to 0.09375
- gain_keys: float32 [512], replicated, may hold values from 0.1 to 1.9
- w_query: bfloat16 [512, 512], P(None, 'ffn'), may hold values from -1.5 to 1.5
- w_key: bfloat16 [512, 512], P(None, 'ffn'), may hold values from -1.5 to 1.5
- w_value: bfloat16 [512, 512], P(None, 'ffn'), may hold values from -0.25 to 0.25
- w_out: bfloat16 [512, 512], P('ffn'), may hold values from -1.796875 to 1.796875
- gain_ffn: float32 [512], replicated, may hold values from 0.1 to 1.9
- w_up: bfloat16 [512, 2048], P(None, 'ffn'), may hold values from -0.25 to 0.25
- w_depth: float32 [27, 2048], P(None, 'ffn'), may hold values from -1.25 to 1.25
- w_down: bfloat16 [2048, 512], P('ffn'), may hold values from -0.125 to 0.125
- grad_out: bfloat16 [32768, 512], P('slab'), may hold values from -0.0625 to 0.0625
Outputs:
- attended: bfloat16 [32768, 512], P('slab')
- grad_up: float32 [512, 2048], P('slab', 'ffn')
- grad_down: float32 [512, 2048], P('slab', 'ffn')
All inputs are finite; a program needn't handle non-finite values.
Results may differ from a plain program's by a relative error of at most 0.024.
The roundings to bfloat16 on the way count: a program that leaves them out, or rounds other values in their place, can miss the bound.
Values may be sent and summed in bfloat16 or wider, within the bound.
A program may use at most 64 MiB of HBM per device.

v0:
```python
import math
import jax
import jax.numpy as jnp
from jax import lax
from jax.sharding import PartitionSpec as P

HEAD = 64
GX = 16
GY = 16
CZ = 2
EPSILON = 1e-05
ROPE_BASE = 100.0
ROOT_HALF = 0.7071067811865476
NORMAL_SCALE = 0.3989422804014327


def padded_2(cells, sides, width):
    for axis, dim in sides:
        count = lax.axis_size(axis)
        ends = count - 1
        head = lax.slice_in_dim(cells, 0, width, axis=dim)
        tail = lax.slice_in_dim(cells, cells.shape[dim] - width, cells.shape[dim], axis=dim)
        cells = jnp.concatenate(
            [
                lax.ppermute(tail, axis, [(i, (i + 1) % count) for i in range(ends)]),
                cells,
                lax.ppermute(head, axis, [((i + 1) % count, i) for i in range(ends)]),
            ],
            axis=dim,
        )
    return cells


def layer_norm(values, scale_gain):
    values = values.astype(jnp.float32)
    centered = values - jnp.mean(values, axis=-1, keepdims=True)
    variance = jnp.mean(centered * centered, axis=-1, keepdims=True)
    return centered * lax.rsqrt(variance + EPSILON) * scale_gain


def rope_tables(coord_x, coord_y, coord_z, head_size):
    pair_count = head_size // 2
    position = jnp.arange(pair_count, dtype=jnp.int32)
    axis_pick = position % 3
    per_axis = (pair_count + 2) // 3
    frequency = ROPE_BASE ** (-(position // 3).astype(jnp.float32) / per_axis)
    angles = (
        coord_x[:, None] * (axis_pick == 0)
        + coord_y[:, None] * (axis_pick == 1)
        + coord_z[:, None] * (axis_pick == 2)
    ) * frequency
    return (jnp.cos(angles)[:, None, :], jnp.sin(angles)[:, None, :])


def token_tables(first_plane, planes, head_size):
    position = jnp.arange(planes * GY * GX, dtype=jnp.int32)
    coord_x = (position % GX).astype(jnp.float32)
    coord_y = (position // GX % GY).astype(jnp.float32)
    coord_z = (first_plane + position // (GX * GY)).astype(jnp.float32)
    return rope_tables(coord_x, coord_y, coord_z, head_size)


def key_tables(first_row, row_count, head_size):
    position = first_row + jnp.arange(row_count, dtype=jnp.int32)
    half_x = GX // 2
    half_y = GY // 2
    coord_x = (position % half_x).astype(jnp.float32) * 2.0 + 0.5
    coord_y = (position // half_x % half_y).astype(jnp.float32) * 2.0 + 0.5
    coord_z = (position // (half_x * half_y)).astype(jnp.float32) * 2.0 + 0.5
    return rope_tables(coord_x, coord_y, coord_z, head_size)


def rotate(values, cosine, sine_table):
    half_size = values.shape[-1] // 2
    front_half = values[..., :half_size]
    back_half = values[..., half_size:]
    return jnp.concatenate(
        [
            front_half * cosine - back_half * sine_table,
            back_half * cosine + front_half * sine_table,
        ],
        axis=-1,
    )


def make_patches(normed, planes):
    width = normed.shape[-1]
    cell_grid = normed.reshape(planes // 2, 2, GY // 2, 2, GX // 2, 2, width)
    return cell_grid.transpose(0, 2, 4, 1, 3, 5, 6).reshape(-1, 8 * width)


def depth_conv(padded, weights, planes):
    height = padded.shape[1] - 2
    width_x = padded.shape[2] - 2
    result = jnp.zeros((planes, height, width_x, padded.shape[3]), jnp.float32)
    for offset in range(27):
        shift_z = offset // 9
        shift_y = offset // 3 % 3
        shift_x = offset % 3
        window = padded[
            shift_z : shift_z + planes, shift_y : shift_y + height, shift_x : shift_x + width_x
        ]
        result = result + window.astype(jnp.float32) * weights[offset]
    return result


def attend_piece(state_tuple, queries, key_rows, value_rows):
    row_max, row_sum, weighted = state_tuple
    score_scale = key_rows.shape[-1] ** (-0.5)
    scores = (
        jnp.einsum("qhd,khd->hqk", queries, key_rows, preferred_element_type=jnp.float32)
        * score_scale
    )
    new_max = jnp.maximum(row_max, jnp.max(scores, axis=2))
    rescale = jnp.exp(row_max - new_max)
    expo = jnp.exp(scores - new_max[:, :, None])
    row_sum = row_sum * rescale + jnp.sum(expo, axis=2)
    weighted = weighted * rescale[:, :, None] + jnp.einsum(
        "hqk,khd->hqd", expo.astype(jnp.bfloat16), value_rows, preferred_element_type=jnp.float32
    )
    return (new_max, row_sum, weighted)


def per_device(
    tokens,
    gain_attn,
    w_reduce,
    gain_keys,
    w_query,
    w_key,
    w_value,
    w_out,
    gain_ffn,
    w_up,
    w_depth,
    w_down,
    grad_out,
):
    slab_index = lax.axis_index("slab")
    tok_rows = tokens.shape[0]
    heads_dev = w_query.shape[1] // HEAD
    normed = layer_norm(tokens, gain_attn).astype(jnp.bfloat16)
    patches = make_patches(normed, CZ)
    reduced = jnp.dot(patches, w_reduce, preferred_element_type=jnp.float32)
    key_input = layer_norm(reduced, gain_keys).astype(jnp.bfloat16)
    tok_cos, tok_sin = token_tables(slab_index * CZ, CZ, HEAD)
    queries = jnp.dot(normed, w_query, preferred_element_type=jnp.float32).reshape(
        tok_rows, heads_dev, HEAD
    )
    queries = rotate(queries, tok_cos, tok_sin).astype(jnp.bfloat16)
    initial = (
        jnp.full((heads_dev, tok_rows), -1e30, jnp.float32),
        jnp.zeros((heads_dev, tok_rows), jnp.float32),
        jnp.zeros((heads_dev, tok_rows, HEAD), jnp.float32),
    )
    state_tuple = initial
    pieces = lax.all_gather(key_input, "slab", axis=0, tiled=True)
    row_count = pieces.shape[0]
    block_rows = math.gcd(row_count, 1024)
    block_count = row_count // block_rows
    blocks = pieces.reshape(block_count, block_rows, pieces.shape[1])

    def one_block(state_inner, block_item):
        rows_in, block_index = block_item
        block_first = block_index * block_rows
        key_cos, key_sin = key_tables(block_first, block_rows, HEAD)
        key_block = jnp.dot(rows_in, w_key, preferred_element_type=jnp.float32).reshape(
            block_rows, heads_dev, HEAD
        )
        key_block = rotate(key_block, key_cos, key_sin).astype(jnp.bfloat16)
        value_block = (
            jnp.dot(rows_in, w_value, preferred_element_type=jnp.float32)
            .astype(jnp.bfloat16)
            .reshape(block_rows, heads_dev, HEAD)
        )
        return (attend_piece(state_inner, queries, key_block, value_block), None)

    state_tuple, _ = lax.scan(
        one_block, state_tuple, (blocks, jnp.arange(block_count, dtype=jnp.int32))
    )
    row_max, row_sum, weighted = state_tuple
    heads_out = (
        (weighted / row_sum[:, :, None])
        .transpose(1, 0, 2)
        .reshape(tok_rows, heads_dev * HEAD)
        .astype(jnp.bfloat16)
    )
    partial_value = jnp.dot(heads_out, w_out, preferred_element_type=jnp.float32)
    head_total = lax.psum(partial_value.astype(jnp.bfloat16), "ffn").astype(jnp.float32)
    attended = head_total.astype(jnp.bfloat16)
    residual = tokens.astype(jnp.float32) + head_total
    normed_ffn = layer_norm(residual, gain_ffn).astype(jnp.bfloat16)
    channels = w_up.shape[1]
    pre = (
        jnp.dot(normed_ffn, w_up, preferred_element_type=jnp.float32)
        .astype(jnp.bfloat16)
        .reshape(CZ, GY, GX, channels)
    )
    pre_wide = padded_2(pre, (("slab", 0),), 1)
    pre_pad = jnp.pad(pre_wide, ((0, 0), (1, 1), (1, 1), (0, 0)))
    mixed = depth_conv(pre_pad, w_depth, CZ).reshape(tok_rows, channels)
    normal_cdf = 0.5 * (1.0 + lax.erf(mixed * ROOT_HALF))
    normal_pdf = jnp.exp(-0.5 * mixed * mixed) * NORMAL_SCALE
    activated = (mixed * normal_cdf).astype(jnp.bfloat16)
    grad_act = jnp.einsum("td,cd->tc", grad_out, w_down, preferred_element_type=jnp.float32)
    grad_mixed = (
        (grad_act * (normal_cdf + mixed * normal_pdf))
        .astype(jnp.bfloat16)
        .reshape(CZ, GY, GX, channels)
    )
    grad_wide = padded_2(grad_mixed, (("slab", 0),), 1)
    grad_pad = jnp.pad(grad_wide, ((0, 0), (1, 1), (1, 1), (0, 0)))
    grad_pre = (
        depth_conv(grad_pad, w_depth[::-1], CZ).astype(jnp.bfloat16).reshape(tok_rows, channels)
    )
    up_full = jnp.einsum("td,tc->dc", normed_ffn, grad_pre, preferred_element_type=jnp.float32)
    down_full = jnp.einsum("td,tc->dc", grad_out, activated, preferred_element_type=jnp.float32)
    grads = lax.psum_scatter(
        jnp.concatenate([up_full, down_full], axis=1), "slab", scatter_dimension=0, tiled=True
    )
    return (attended, grads[:, :channels], grads[:, channels:])


def solution(mesh):
    in_specs = (
        P("slab", None),
        P(),
        P(),
        P(),
        P(None, "ffn"),
        P(None, "ffn"),
        P(None, "ffn"),
        P("ffn", None),
        P(),
        P(None, "ffn"),
        P(None, "ffn"),
        P("ffn", None),
        P("slab", None),
    )
    out_specs = (P("slab", None), P("slab", "ffn"), P("slab", "ffn"))
    return jax.shard_map(
        per_device, mesh=mesh, in_specs=in_specs, out_specs=out_specs, check_vma=False
    )
```

profile of v0, /device:TPU:4, one launch (start us, length us, event | category | flops | bytes accessed | tf_op | source)
XLA Modules:
  0.0 795.7 jit_solution(1866074170113802012)
XLA Ops:
  12.2 3.2 fusion.96
  17.3 306.8 %all-gather.2.cloned.1.call-done = bf16[4096,512]{1,0:T(8,128)(2,1)} async-done(((bf16[64,512]{1,0:T(8,128)(2,1)}), bf16[4096,512]{1,0:T(8,128)(2,1)}) %all-gather.2.cloned.1.call-update) | async-done | bytes 4194320 | tf_op jit(solution)/shard_map/all_gather | solution.py:157
  324.1 48.4 %while.18 = (s32[]{:T(128)}, f32[2,512]{1,0:T(2,128)S(1)}, f32[2,512]{1,0:T(2,128)S(1)}, f32[2,512,64]{1,2,0:T(8,128)S(1)}, bf16[4,1024,512]{2,1,0:T(8,128)(2,1)...) while((s32[]{:T(128)}, f32[2,512]{1,0:T(2,128)S(1)}, ...), condition=%wide.region_7.8_spmd.clone, body=%wide.region_4.7_spmd.clone.sunk | while | flops 546895744 | bytes 35088572 | solution.py:178
  326.0 1.7 fusion.137
  327.8 2.7 bitcast_reduce_fusion.2
  330.5 3.0 fusion.143
  333.6 1.7 convolution_convert_fusion.4
  338.1 1.7 fusion.137
  339.9 2.7 bitcast_reduce_fusion.2
  342.6 3.0 fusion.143
  345.7 1.7 convolution_convert_fusion.4
  350.2 1.7 fusion.137
  352.0 2.7 bitcast_reduce_fusion.2
  354.7 3.0 fusion.143
  357.8 1.7 convolution_convert_fusion.4
  362.3 1.7 fusion.137
  364.1 2.7 bitcast_reduce_fusion.2
  366.9 3.0 fusion.143
  369.9 1.7 convolution_convert_fusion.4
  373.8 41.8 %all-reduce.4.cloned.1.call-done = bf16[512,512]{1,0:T(8,128)(2,1)} async-done(((bf16[512,512]{1,0:T(8,128)(2,1)}), bf16[512,512]{1,0:T(8,128)(2,1)}) %all-reduce.4.cloned.1.call-update) | async-done | bytes 524304 | tf_op jit(solution)/shard_map/psum | solution.py:189
  418.2 1.6 convolution_convert_fusion.1
  419.9 3.7 collective-permute-start
  425.0 10.3 %collective-permute-done = bf16[1,16,16,512]{3,2,1,0:T(8,128)(2,1)S(1)} collective-permute-done((bf16[1,16,16,512]{3,2,1,0:T(8,128)(2,1)S(1)}, bf16[1,16,16,512]{3,2,1,0:T(8,128)(2,1)S(1)}, u32[]{:S(2)}, u32[]{:S(2)}) %collective-permute-start) | collective-permute-done | bytes 262176 | tf_op jit(solution)/shard_map/ppermute | solution.py:25
  435.2 3.5 collective-permute-done.1
  439.5 3.8 multiply_add_fusion
  444.2 1.5 collective-permute-start.2
  445.7 1.5 collective-permute-start.3
  447.7 9.5 %collective-permute-done.2 = bf16[1,16,16,512]{3,2,1,0:T(8,128)(2,1)S(1)} collective-permute-done((bf16[1,16,16,512]{3,2,1,0:T(8,128)(2,1)S(1)}, bf16[1,16,16,512]{3,2,1,0:T(8,128)(2,1)S(1)}, u32[]{:S(2)}, u32[]{:S(2)}) %collective-permute-start.2) | collective-permute-done | bytes 262176 | tf_op jit(solution)/shard_map/ppermute | solution.py:25
  457.2 4.1 collective-permute-done.3
  462.1 3.8 add_convert_fusion.1
  466.8 1.8 copy.31
  468.7 318.3 %reduce-scatter.4.cloned.1.call-done = f32[8,1024]{1,0:T(8,128)} async-done(((f32[512,1024]{1,0:T(8,128)}), f32[8,1024]{1,0:T(8,128)}) %reduce-scatter.4.cloned.1.call-update) | async-done | bytes 32784
  (134 shorter events, 26.5 us)
Async XLA Ops:
  7.2 436.4 %copy-start = (bf16[512,512]{1,0:T(8,128)(2,1)S(1)}, bf16[512,512]{1,0:T(8,128)(2,1)}, u32[]{:S(2)}) copy-start(bf16[512,512]{1,0:T(8,128)(2,1)} %param.27) | copy-start | bytes 1572868
  7.2 316.9 %all-gather.2.cloned.1.call-start = ((), (), s32[]{:S(2)}) async-start(), calls=%async_computation.1 | async-start | bytes 4259840 | tf_op jit(solution)/shard_map/all_gather | solution.py:157
  11.3 4.2 copy-start.11
  11.3 5.1 copy-start.8
  11.7 5.2 copy-start.7
  12.1 311.9 %copy-start.5 = (bf16[512,128]{1,0:T(8,128)(2,1)S(1)}, bf16[512,128]{1,0:T(8,128)(2,1)}, u32[]{:S(2)}) copy-start(bf16[512,128]{1,0:T(8,128)(2,1)} %param.21) | copy-start | bytes 393220
  16.3 399.3 %all-reduce.4.cloned.1.call-start = ((), (), s32[]{:S(2)}) async-start(), calls=%async_computation.2 | async-start | bytes 1048576 | tf_op jit(solution)/shard_map/psum | solution.py:189
  324.1 48.5 %copy-start.9 = (bf16[128,512]{1,0:T(8,128)(2,1)S(1)}, bf16[128,512]{1,0:T(8,128)(2,1)}, u32[]{:S(2)}) copy-start(bf16[128,512]{1,0:T(8,128)(2,1)} %param.22) | copy-start | bytes 393220
  324.1 91.5 %copy-start.2 = (bf16[512,512]{1,0:T(8,128)(2,1)S(1)}, bf16[512,512]{1,0:T(8,128)(2,1)}, u32[]{:S(2)}) copy-start(bf16[512,512]{1,0:T(8,128)(2,1)} %param.15) | copy-start | bytes 1572868
  330.5 4.8 copy-start.1
  342.6 4.8 copy-start.1
  354.7 4.8 copy-start.1
  366.8 4.8 copy-start.1
  372.5 45.7 %copy-start.12 = (bf16[512,512]{1,0:T(8,128)(2,1)S(1)}, bf16[512,512]{1,0:T(8,128)(2,1)}, u32[]{:S(2)}) copy-start(bf16[512,512]{1,0:T(8,128)(2,1)} %param.24) | copy-start | bytes 1572868
  372.5 45.7 %copy-start.13 = (f32[512]{0:T(512)S(1)}, f32[512]{0:T(512)}, u32[]{:S(2)}) copy-start(f32[512]{0:T(512)} %param.23) | copy-start | bytes 6148
  372.6 52.3 %copy-start.10 = (f32[27,512]{1,0:T(8,128)S(1)}, f32[27,512]{1,0:T(8,128)}, u32[]{:S(2)}) copy-start(f32[27,512]{1,0:T(8,128)} %param.25) | copy-start | bytes 165892
  373.8 413.3 %reduce-scatter.4.cloned.1.call-start = ((), (), s32[]{:S(2)}) async-start(), calls=%async_computation.3 | async-start | bytes 2129920
  419.9 15.4 %collective-permute-start = (bf16[1,16,16,512]{3,2,1,0:T(8,128)(2,1)S(1)}, bf16[1,16,16,512]{3,2,1,0:T(8,128)(2,1)S(1)}, u32[]{:S(2)}, u32[]{:S(2)}) collective-permute-start(bf16[1,16,16,512]{3,2,1,0:T(8,128)(2,1)S(1)} %bitcast.133), channel_id=1, source_target_pairs={{0,4},{4,8},{8,12},{12,16},{16,20},{20,24},{24,28},{28,32},{32,36}... | collective-permute-start | bytes 786440 | tf_op jit(solution)/shard_map/ppermute | solution.py:25
  423.6 15.2 %collective-permute-start.1 = (bf16[1,16,16,512]{3,2,1,0:T(8,128)(2,1)S(1)}, bf16[1,16,16,512]{3,2,1,0:T(8,128)(2,1)S(1)}, u32[]{:S(2)}, u32[]{:S(2)}) collective-permute-start(bf16[1,16,16,512]{3,2,1,0:T(8,128)(2,1)S(1)} %bitcast.132), channel_id=1, source_target_pairs={{4,0},{8,4},{12,8},{16,12},{20,16},{24,20},{28,24},{32,28},{36,32}... | collective-permute-start | bytes 786440 | tf_op jit(solution)/shard_map/ppermute | solution.py:27
  439.5 4.1 copy-start.6
  444.2 12.9 %collective-permute-start.2 = (bf16[1,16,16,512]{3,2,1,0:T(8,128)(2,1)S(1)}, bf16[1,16,16,512]{3,2,1,0:T(8,128)(2,1)S(1)}, u32[]{:S(2)}, u32[]{:S(2)}) collective-permute-start(bf16[1,16,16,512]{3,2,1,0:T(8,128)(2,1)S(1)} %bitcast.135), channel_id=1, source_target_pairs={{0,4},{4,8},{8,12},{12,16},{16,20},{20,24},{24,28},{28,32},{32,36}... | collective-permute-start | bytes 786440 | tf_op jit(solution)/shard_map/ppermute | solution.py:25
  445.7 15.6 %collective-permute-start.3 = (bf16[1,16,16,512]{3,2,1,0:T(8,128)(2,1)S(1)}, bf16[1,16,16,512]{3,2,1,0:T(8,128)(2,1)S(1)}, u32[]{:S(2)}, u32[]{:S(2)}) collective-permute-start(bf16[1,16,16,512]{3,2,1,0:T(8,128)(2,1)S(1)} %bitcast.134), channel_id=1, source_target_pairs={{4,0},{8,4},{12,8},{16,12},{20,16},{24,20},{28,24},{32,28},{36,32}... | collective-permute-start | bytes 786440 | tf_op jit(solution)/shard_map/ppermute | solution.py:27
  462.1 3.9 copy-start.3
  466.8 321.6 %copy-start.4 = (bf16[512,512]{1,0:T(8,128)(2,1)S(1)}, bf16[512,512]{1,0:T(8,128)(2,1)}, u32[]{:S(2)}) copy-start(bf16[512,512]{1,0:T(8,128)(2,1)} %all-reduce.4.cloned.1.call-done) | copy-start | bytes 1572868
Sparse Core Ops, SparseCore 0:
  16.4 307.6 all-gather.1
  373.9 41.6 all-reduce.3
  468.8 318.1 reduce-scatter.3
where the time goes:
time: 796 us
  waiting for transfers between devices  694 us (87%)
  matrix products  35.8 us (4%)
  other arithmetic  32.5 us (4%)
  between operations  14.2 us (2%)
  starting transfers between devices  8.07 us (1%)
    unnamed x4, waiting for transfers between devices  318 us
    all_gather x1, waiting for transfers between devices, per_device(): pieces = lax.all_gather(key_input, 'slab', axis=0, tiled=True)  307 us
    psum x1, waiting for transfers between devices, per_device(): lax.psum(partial_value.astype(jnp.bfloat16), 'ffn').astype(jnp.float32)  41.8 us
    ppermute x2, waiting for transfers between devices, padded_2(): lax.ppermute(tail, axis, [(i, (i + 1) % count) for i in range(ends)])  19.8 us
  transfers between devices with their start and end apart: 7, of which 7 were waited for; matrix products, arithmetic and copies ran while one was open for 0% of the time, Pallas kernels for 0%

commit v1 on v0

--- a/solution.py
+++ b/solution.py
@@ -154,7 +154,10 @@
         jnp.zeros((heads_dev, tok_rows, HEAD), jnp.float32),
     )
     state_tuple = initial
-    pieces = lax.all_gather(key_input, "slab", axis=0, tiled=True)
+    n_dev = lax.axis_size("slab")
+    parts = jnp.stack([key_input for _ in range(n_dev)])
+    parts = lax.all_to_all(parts, "slab", split_axis=0, concat_axis=0)
+    pieces = jnp.concatenate(parts, axis=0)
     row_count = pieces.shape[0]
     block_rows = math.gcd(row_count, 1024)
     block_count = row_count // block_rows

time: 796 us -> 600 us (0.75)
  waiting for transfers between devices: 694 us -> 483 us
  starting transfers between devices: 8.07 us -> 21.2 us
    all_gather x1 -> x0, waiting for transfers between devices: 307 us -> none  [per_device(): pieces = lax.all_gather(key_input, 'slab', axis=0, tiled=True)]
    all_to_all x0 -> x1, waiting for transfers between devices: none -> 95.1 us  [per_device(): parts = lax.all_to_all(parts, 'slab', split_axis=0, concat_axis=0)]
    all_to_all x0 -> x1, starting transfers between devices: none -> 13.1 us  [per_device(): parts = lax.all_to_all(parts, 'slab', split_axis=0, concat_axis=0)]
    unnamed x4 -> x3, waiting for transfers between devices: 318 us -> 319 us
where the time goes in v1:
time: 600 us; the launch traced here: 599 us
  waiting for transfers between devices  483 us (80%)
  matrix products  35.8 us (6%)
  other arithmetic  31.9 us (5%)
  starting transfers between devices  21.2 us (4%)
  between operations  14.5 us (2%)
  local copies, waits for them, and re-layouts  10.1 us (2%)
    unnamed x3, waiting for transfers between devices  319 us
    all_to_all x1, waiting for transfers between devices, per_device(): parts = lax.all_to_all(parts, 'slab', split_axis=0, concat_axis=0)  95.1 us
    psum x1, waiting for transfers between devices, per_device(): lax.psum(partial_value.astype(jnp.bfloat16), 'ffn').astype(jnp.float32)  41.4 us
    ppermute x2, waiting for transfers between devices, padded_2(): lax.ppermute(tail, axis, [(i, (i + 1) % count) for i in range(ends)])  19.8 us
    all_to_all x1, starting transfers between devices, per_device(): parts = lax.all_to_all(parts, 'slab', split_axis=0, concat_axis=0)  13.1 us
    reduce_sum x4, other arithmetic, attend_piece(): row_sum = row_sum * rescale + jnp.sum(expo, axis=2)  12.2 us
  transfers between devices with their start and end apart: 7, of which 7 were waited for; matrix products, arithmetic and copies ran while one was open for 0% of the time, Pallas kernels for 0%

profile of v1, /device:TPU:4, one launch (start us, length us, event | category | flops | bytes accessed | tf_op | source)
XLA Modules:
  0.0 599.1 jit_solution(6627243439894677014)
XLA Ops:
  12.1 3.1 fusion.96
  15.5 2.5 stack.2
  18.0 13.1 %all-to-all-start = ((bf16[64,64,512]{2,1,0:T(8,128)(2,1)}), bf16[64,64,512]{2,1,0:T(8,128)(2,1)}, u32[]{:S(2)}, u32[]{:S(2)}) async-start(bf16[64,64,512]{2,1,0:T(8,128)(2,1)} %stack.2), calls=%async_computation | async-start | bytes 8388608 | tf_op jit(solution)/shard_map/all_to_all | solution.py:159
  32.2 95.1 %all-to-all-done = bf16[64,64,512]{2,1,0:T(8,128)(2,1)} async-done(((bf16[64,64,512]{2,1,0:T(8,128)(2,1)}), bf16[64,64,512]{2,1,0:T(8,128)(2,1)}, u32[]{:S(2)}, u32[]{:S(2)}) %all-to-all-start) | async-done | bytes 4194336 | tf_op jit(solution)/shard_map/all_to_all | solution.py:159
  127.3 48.4 %while.18 = (s32[]{:T(128)}, f32[2,512]{1,0:T(2,128)S(1)}, f32[2,512]{1,0:T(2,128)S(1)}, f32[2,512,64]{1,2,0:T(8,128)S(1)}, bf16[4,1024,512]{2,1,0:T(8,128)(2,1)...) while((s32[]{:T(128)}, f32[2,512]{1,0:T(2,128)S(1)}, ...), condition=%wide.region_7.8_spmd.clone, body=%wide.region_4.7_spmd.clone.sunk | while | flops 546895744 | bytes 35088572 | solution.py:181
  129.2 1.7 fusion.137
  131.0 2.7 bitcast_reduce_fusion.2
  133.7 3.0 fusion.143
  136.8 1.7 convolution_convert_fusion.4
  141.3 1.7 fusion.137
  143.1 2.7 bitcast_reduce_fusion.2
  145.8 3.0 fusion.143
  148.9 1.7 convolution_convert_fusion.4
  153.4 1.7 fusion.137
  155.2 2.7 bitcast_reduce_fusion.2
  157.9 3.0 fusion.143
  161.0 1.7 convolution_convert_fusion.4
  165.5 1.7 fusion.137
  167.3 2.7 bitcast_reduce_fusion.2
  170.1 3.0 fusion.143
  173.1 1.7 convolution_convert_fusion.4
  177.0 41.4 %all-reduce.4.cloned.1.call-done = bf16[512,512]{1,0:T(8,128)(2,1)} async-done(((bf16[512,512]{1,0:T(8,128)(2,1)}), bf16[512,512]{1,0:T(8,128)(2,1)}) %all-reduce.4.cloned.1.call-update) | async-done | bytes 524304 | tf_op jit(solution)/shard_map/psum | solution.py:192
  221.0 1.6 convolution_convert_fusion.1
  222.6 3.7 collective-permute-start
  227.9 10.1 %collective-permute-done = bf16[1,16,16,512]{3,2,1,0:T(8,128)(2,1)S(1)} collective-permute-done((bf16[1,16,16,512]{3,2,1,0:T(8,128)(2,1)S(1)}, bf16[1,16,16,512]{3,2,1,0:T(8,128)(2,1)S(1)}, u32[]{:S(2)}, u32[]{:S(2)}) %collective-permute-start) | collective-permute-done | bytes 262176 | tf_op jit(solution)/shard_map/ppermute | solution.py:25
  238.0 3.5 collective-permute-done.1
  242.3 3.8 multiply_add_fusion
  250.3 9.7 %collective-permute-done.2 = bf16[1,16,16,512]{3,2,1,0:T(8,128)(2,1)S(1)} collective-permute-done((bf16[1,16,16,512]{3,2,1,0:T(8,128)(2,1)S(1)}, bf16[1,16,16,512]{3,2,1,0:T(8,128)(2,1)S(1)}, u32[]{:S(2)}, u32[]{:S(2)}) %collective-permute-start.2) | collective-permute-done | bytes 262176 | tf_op jit(solution)/shard_map/ppermute | solution.py:25
  260.0 4.1 collective-permute-done.3
  264.9 3.8 add_convert_fusion.1
  269.6 1.8 copy.31
  271.4 318.7 %reduce-scatter.4.cloned.1.call-done = f32[8,1024]{1,0:T(8,128)} async-done(((f32[512,1024]{1,0:T(8,128)}), f32[8,1024]{1,0:T(8,128)}) %reduce-scatter.4.cloned.1.call-update) | async-done | bytes 32784
  (134 shorter events, 28.8 us)
Async XLA Ops:
  7.2 239.2 %copy-start = (bf16[512,512]{1,0:T(8,128)(2,1)S(1)}, bf16[512,512]{1,0:T(8,128)(2,1)}, u32[]{:S(2)}) copy-start(bf16[512,512]{1,0:T(8,128)(2,1)} %param.27) | copy-start | bytes 1572868
  11.3 4.2 copy-start.11
  18.0 13.2 %copy-start.8 = (bf16[512,128]{1,0:T(8,128)(2,1)S(1)}, bf16[512,128]{1,0:T(8,128)(2,1)}, u32[]{:S(2)}) copy-start(bf16[512,128]{1,0:T(8,128)(2,1)} %param.20) | copy-start | bytes 393220
  18.0 13.8 %copy-start.7 = (bf16[512,128]{1,0:T(8,128)(2,1)S(1)}, bf16[512,128]{1,0:T(8,128)(2,1)}, u32[]{:S(2)}) copy-start(bf16[512,128]{1,0:T(8,128)(2,1)} %param.19) | copy-start | bytes 393220
  18.0 109.3 %copy-start.5 = (bf16[512,128]{1,0:T(8,128)(2,1)S(1)}, bf16[512,128]{1,0:T(8,128)(2,1)}, u32[]{:S(2)}) copy-start(bf16[512,128]{1,0:T(8,128)(2,1)} %param.21) | copy-start | bytes 393220
  18.0 109.3 %all-to-all-start = ((bf16[64,64,512]{2,1,0:T(8,128)(2,1)}), bf16[64,64,512]{2,1,0:T(8,128)(2,1)}, u32[]{:S(2)}, u32[]{:S(2)}) async-start(bf16[64,64,512]{2,1,0:T(8,128)(2,1)} %stack.2), calls=%async_computation | async-start | bytes 8388608 | tf_op jit(solution)/shard_map/all_to_all | solution.py:159
  31.2 187.2 %all-reduce.4.cloned.1.call-start = ((), (), s32[]{:S(2)}) async-start(), calls=%async_computation.2 | async-start | bytes 1048576 | tf_op jit(solution)/shard_map/psum | solution.py:192
  127.3 48.5 %copy-start.9 = (bf16[128,512]{1,0:T(8,128)(2,1)S(1)}, bf16[128,512]{1,0:T(8,128)(2,1)}, u32[]{:S(2)}) copy-start(bf16[128,512]{1,0:T(8,128)(2,1)} %param.22) | copy-start | bytes 393220
  127.3 91.1 %copy-start.2 = (bf16[512,512]{1,0:T(8,128)(2,1)S(1)}, bf16[512,512]{1,0:T(8,128)(2,1)}, u32[]{:S(2)}) copy-start(bf16[512,512]{1,0:T(8,128)(2,1)} %param.15) | copy-start | bytes 1572868
  133.7 4.8 copy-start.1
  145.8 4.8 copy-start.1
  157.9 4.8 copy-start.1
  170.0 4.8 copy-start.1
  175.7 45.3 %copy-start.12 = (bf16[512,512]{1,0:T(8,128)(2,1)S(1)}, bf16[512,512]{1,0:T(8,128)(2,1)}, u32[]{:S(2)}) copy-start(bf16[512,512]{1,0:T(8,128)(2,1)} %param.24) | copy-start | bytes 1572868
  175.7 45.3 %copy-start.13 = (f32[512]{0:T(512)S(1)}, f32[512]{0:T(512)}, u32[]{:S(2)}) copy-start(f32[512]{0:T(512)} %param.23) | copy-start | bytes 6148
  175.8 52.1 %copy-start.10 = (f32[27,512]{1,0:T(8,128)S(1)}, f32[27,512]{1,0:T(8,128)}, u32[]{:S(2)}) copy-start(f32[27,512]{1,0:T(8,128)} %param.25) | copy-start | bytes 165892
  176.9 413.2 %reduce-scatter.4.cloned.1.call-start = ((), (), s32[]{:S(2)}) async-start(), calls=%async_computation.3 | async-start | bytes 2129920
  222.6 15.4 %collective-permute-start = (bf16[1,16,16,512]{3,2,1,0:T(8,128)(2,1)S(1)}, bf16[1,16,16,512]{3,2,1,0:T(8,128)(2,1)S(1)}, u32[]{:S(2)}, u32[]{:S(2)}) collective-permute-start(bf16[1,16,16,512]{3,2,1,0:T(8,128)(2,1)S(1)} %bitcast.132), channel_id=1, source_target_pairs={{0,4},{4,8},{8,12},{12,16},{16,20},{20,24},{24,28},{28,32},{32,36}... | collective-permute-start | bytes 786440 | tf_op jit(solution)/shard_map/ppermute | solution.py:25
  226.4 15.2 %collective-permute-start.1 = (bf16[1,16,16,512]{3,2,1,0:T(8,128)(2,1)S(1)}, bf16[1,16,16,512]{3,2,1,0:T(8,128)(2,1)S(1)}, u32[]{:S(2)}, u32[]{:S(2)}) collective-permute-start(bf16[1,16,16,512]{3,2,1,0:T(8,128)(2,1)S(1)} %bitcast.131), channel_id=1, source_target_pairs={{4,0},{8,4},{12,8},{16,12},{20,16},{24,20},{28,24},{32,28},{36,32}... | collective-permute-start | bytes 786440 | tf_op jit(solution)/shard_map/ppermute | solution.py:27
  242.3 4.1 copy-start.6
  247.0 12.9 %collective-permute-start.2 = (bf16[1,16,16,512]{3,2,1,0:T(8,128)(2,1)S(1)}, bf16[1,16,16,512]{3,2,1,0:T(8,128)(2,1)S(1)}, u32[]{:S(2)}, u32[]{:S(2)}) collective-permute-start(bf16[1,16,16,512]{3,2,1,0:T(8,128)(2,1)S(1)} %bitcast.134), channel_id=1, source_target_pairs={{0,4},{4,8},{8,12},{12,16},{16,20},{20,24},{24,28},{28,32},{32,36}... | collective-permute-start | bytes 786440 | tf_op jit(solution)/shard_map/ppermute | solution.py:25
  248.5 15.6 %collective-permute-start.3 = (bf16[1,16,16,512]{3,2,1,0:T(8,128)(2,1)S(1)}, bf16[1,16,16,512]{3,2,1,0:T(8,128)(2,1)S(1)}, u32[]{:S(2)}, u32[]{:S(2)}) collective-permute-start(bf16[1,16,16,512]{3,2,1,0:T(8,128)(2,1)S(1)} %bitcast.133), channel_id=1, source_target_pairs={{4,0},{8,4},{12,8},{16,12},{20,16},{24,20},{28,24},{32,28},{36,32}... | collective-permute-start | bytes 786440 | tf_op jit(solution)/shard_map/ppermute | solution.py:27
  264.9 3.9 copy-start.3
  269.6 321.9 %copy-start.4 = (bf16[512,512]{1,0:T(8,128)(2,1)S(1)}, bf16[512,512]{1,0:T(8,128)(2,1)}, u32[]{:S(2)}) copy-start(bf16[512,512]{1,0:T(8,128)(2,1)} %all-reduce.4.cloned.1.call-done) | copy-start | bytes 1572868
Sparse Core Ops, SparseCore 0:
  177.1 41.2 all-reduce.3
  271.6 318.5 reduce-scatter.3
